TPU v7x, 256 devices: a whole 4x4x8 slice. The times are simulated.
256 devices in a mesh: tm: 256 (over z, x, y, core).
Axes of the slice: x: 4, y: 4, z: 8, core: 2. Of those that a mesh axis runs over, the one named last changes fastest.
Arguments:
- transition: float32 [256, 256], replicated, may hold values from -1 to 1
- noise_var: float32 [256], replicated, may hold values from 0.001 to 0.1
- prior_mean: float32 [256], replicated, may hold values from -6 to 6
- prior_var: float32 [256], replicated, may hold values from 0.5 to 2
- obs_op: bfloat16 [256, 8, 128, 128], P('tm'), may hold values from -0.5 to 0.5
- obs_value: float32 [256, 8, 128], P('tm'), may hold values from -18 to 18
- obs_noise: float32 [256, 8, 128], P('tm'), may hold values from 10 to 100
- obs_block: int32 [256, 8], P('tm'), may hold values from 0 to 1
- obs_count: int32 [256], P('tm'), may hold values from 1 to 8, as said below
Outputs:
- smoothed_mean: float32 [256, 256], P('tm')
- smoothed_var: float32 [256, 256], P('tm')
Inputs may be any that keep to these rules, and one draw needn't show every extreme that they name: Only the first obs_count[t] slots of step t carry observations; some step reports all 8.
All inputs are finite; a program needn't handle non-finite values.
Results may differ from a plain program's by a relative error of at most 0.024.
Values sent between devices are 32-bit elements; how exact they have to be, the bound alone decides.
No kernel may reach another device: no remote copies, remote signals or barrier semaphores. Data moves between devices by JAX's collectives and lax.ppermute only.
A program may use at most 192 MiB of HBM per device.

v0:
```python
import functools

import jax
import jax.numpy as jnp
from jax import lax
from jax.experimental import pallas as pl
from jax.experimental.pallas import tpu as pltpu
from jax.sharding import PartitionSpec as P

f32 = jnp.float32
bf16 = jnp.bfloat16


def halves(value):
    high = value.astype(bf16)
    return high, (value - high.astype(f32)).astype(bf16)


ROWS = ((1,), (0,))
TURNED = ((1,), (1,))


def mul_halves(left, right, contract=ROWS):
    dims = (contract, ((), ()))
    a, b = left
    c, d = right
    rows = a.shape[0]
    both = lax.dot_general(jnp.concatenate([a, b], axis=0), c, dims, preferred_element_type=f32)
    return both[0:rows] + (both[rows:] + lax.dot_general(a, d, dims, preferred_element_type=f32))


def mul(left, right):
    return mul_halves(halves(left), halves(right))


def mul_nt(left, right):
    return mul_halves(halves(left), halves(right), TURNED)


def stack(*parts):
    return tuple(jnp.concatenate(group, axis=0) for group in zip(*parts))


def masks(size):
    rows = lax.broadcasted_iota(jnp.int32, (size, size), 0)
    cols = lax.broadcasted_iota(jnp.int32, (size, size), 1)
    return rows > cols, rows == cols


def rows8(vector):
    return jnp.broadcast_to(vector, (8, vector.shape[1]))


def invert(m, work):
    size = m.shape[0]
    _, diag = masks(size)
    eye = diag.astype(f32)
    magnitude = jnp.abs(m)
    bound = jnp.max(jnp.sum(magnitude, axis=0, keepdims=True))
    scale = 2.0 / (2.0 + bound)
    work[0:size] = scale * eye
    work[size : 2 * size] = (1.0 - scale) * eye - scale * m

    def step(radius):
        square = radius * radius
        factor = 2.0 / (2.0 - square)
        whole = work[...]
        lower = whole[size : 2 * size]
        ends = jnp.where(diag, lower, 0.0)
        across = jnp.sum(ends, axis=0, keepdims=True)
        down = jnp.sum(ends, axis=1, keepdims=True)
        low = whole.astype(bf16)
        rest = lower - ends
        rest_low = rest.astype(bf16)
        out = jnp.dot(
            jnp.concatenate([low[0:size], rest_low], axis=0), rest_low, preferred_element_type=f32
        )
        work[0:size] = factor * (whole[0:size] * (1.0 + across) + out[0:size])
        work[size : 2 * size] = factor * (
            out[size : 2 * size] + lower * across + rest * down
        ) + (1.0 - factor) * eye
        return square / (2.0 - square)

    lax.while_loop(
        lambda radius: radius > 2e-2, step, jnp.minimum(bound / (2.0 + bound), 1.0 - 1e-6)
    )
    split = halves(m)

    def more(carry):
        square_of, count = carry
        return jnp.logical_and(square_of > 2e-3, count < 60)

    def correct(carry):
        _, count = carry
        x = work[0:size]
        x_halves = halves(x)
        residual = eye - x - mul_halves(x_halves, split)
        low = residual.astype(bf16)
        square = jnp.dot(low, low, preferred_element_type=f32)
        square_of = jnp.max(jnp.sum(jnp.abs(square), axis=0, keepdims=True))
        bad = jnp.logical_and(count == 0, jnp.logical_not(square_of < 0.25))
        better = x + mul_halves(halves(residual + square), x_halves)
        work[0:size] = jnp.where(bad, scale * eye, better)
        return jnp.where(bad, 1.0, square_of), count + 1

    lax.while_loop(more, correct, (jnp.float32(1.0), jnp.int32(0)))
    return work[0:size]


def unpack(tail, linear, square):
    below, diag = masks(square.shape[0])
    turned = square.T
    upto = jnp.logical_or(below, diag)
    info = jnp.where(upto, square, turned)
    cov = jnp.where(upto, turned, square)
    cov = jnp.where(diag, tail[2:3], cov)
    return linear, tail[0:1], cov, tail[1:2], info


def unpack_whole(ref):
    size = ref.shape[1]
    return unpack(ref[0:8], ref[8 : size + 8], ref[size + 8 : 2 * size + 8])


def unpack_halves(got, far, core):
    size = got.shape[1]
    swap = core == 1
    own = got[...]
    other = far[...]
    head = jnp.where(swap, other, own)
    square = jnp.where(swap, own[8:], other[8:])
    return unpack(head[0:8], head[8:], square)


def dual(flag, element):
    linear, offset, cov, vector, info = element
    return (
        jnp.where(flag, linear.T, linear),
        jnp.where(flag, vector, offset),
        jnp.where(flag, info, cov),
        jnp.where(flag, -offset, vector),
        jnp.where(flag, cov, info),
    )


def ordered(flag, one, two):
    return (
        [jnp.where(flag, b, a) for a, b in zip(one, two)],
        [jnp.where(flag, a, b) for a, b in zip(one, two)],
    )


def pack(linear, offset, cov, vector, info):
    size = cov.shape[0]
    below, diag = masks(size)
    square = jnp.where(jnp.logical_or(below, diag), info, cov)
    diagonal = jnp.sum(jnp.where(diag, cov, 0.0), axis=0, keepdims=True)
    tail = jnp.concatenate([offset, vector, diagonal, jnp.zeros((5, size), f32)], axis=0)
    return jnp.concatenate([tail, linear, square], axis=0)


def fold(first, second, work):
    lin1, off1, cov1, vec1, inf1 = first
    lin2, off2, cov2, vec2, inf2 = second
    size = cov1.shape[0]
    cov1_halves = halves(cov1)
    lin1_halves = halves(lin1)
    lin2_halves = halves(lin2)
    inf2_halves = halves(inf2)
    top = mul_halves(stack(cov1_halves, halves(rows8(off1))), inf2_halves)
    pull = halves(rows8(vec2 - top[size : size + 1]))
    weight = halves(invert(top[0:size], work[0]))
    moved = halves(mul_halves(stack(lin2_halves, inf2_halves, pull), weight))
    lin_halves = tuple(part[0:size] for part in moved)
    left = mul_halves(moved, lin1_halves)
    spread = mul_halves(stack(lin_halves, halves(rows8(vec2))), cov1_halves)
    push = off1 + spread[size : size + 1]
    info = inf1 + mul(lin1.T, left[size : 2 * size])
    cov = cov2 + mul_halves(halves(spread[0:size]), lin2_halves, TURNED)
    offset = off2 + mul_halves(halves(rows8(push)), lin_halves, TURNED)[0:1]
    return left[0:size], offset, cov, vec1 + left[2 * size : 2 * size + 1], info


def half_fold(cov1, off1, second, work):
    lin2, off2, cov2, vec2, inf2 = second
    size = cov1.shape[0]
    cov1_halves = halves(cov1)
    lin2_halves = halves(lin2)
    weight = invert(mul_halves(cov1_halves, halves(inf2)), work[0])
    lin_halves = halves(mul_halves(lin2_halves, halves(weight)))
    spread = mul_halves(stack(lin_halves, halves(rows8(vec2))), cov1_halves)
    push = off1 + spread[size : size + 1]
    cov = cov2 + mul_halves(halves(spread[0:size]), lin2_halves, TURNED)
    offset = off2 + mul_halves(halves(rows8(push)), lin_halves, TURNED)[0:1]
    return cov, offset


def build_kernel(flags, trans, op_ref, rows, out, info_ref, work):
    slots, stations, width = op_ref.shape
    size = trans.shape[0]
    step = flags[0]
    value = rows[0:slots]
    noise = rows[slots : 2 * slots]

    def row(index):
        at = 2 * slots + 2 * index
        return jnp.concatenate([rows[at : at + 1], rows[at + 1 : at + 2]], axis=1)

    var_row, mean_row, start_row = row(0), row(1), row(2)
    count = rows[2 * slots + 6 : 2 * slots + 7, 0:1]
    blocks = rows[2 * slots + 7 : 2 * slots + 8]
    noise_cols = noise.T
    weighted = value / noise
    info_ref[...] = jnp.zeros(info_ref.shape, f32)
    infos = [jnp.zeros((width, width), f32) for _ in range(size // width)]
    shifts = [jnp.zeros((1, width), f32) for _ in range(size // width)]
    for m in range(slots):
        op = op_ref[m]
        scaled = (op.astype(f32) / noise_cols[:, m : m + 1]).astype(bf16)
        part = lax.dot_general(scaled, op, (((0,), (0,)), ((), ())), preferred_element_type=f32)
        both = jnp.concatenate(halves(rows8(weighted[m : m + 1])), axis=0)
        both = jnp.dot(both, op, preferred_element_type=f32)
        shift = both[0:1] + both[8:9]
        for a in range(size // width):
            keep = jnp.logical_and(count > m, blocks[:, m : m + 1] == a).astype(f32)
            infos[a] = infos[a] + keep * part
            shifts[a] = shifts[a] + keep * shift
    for a, info in enumerate(infos):
        info = 0.5 * (info + info.T)
        info_ref[a * width : (a + 1) * width, a * width : (a + 1) * width] = info
    h = jnp.concatenate(shifts, axis=1)
    info = info_ref[...]
    first = (step == 0).astype(f32)
    var = first * start_row + (1.0 - first) * var_row
    mean = first * mean_row
    moving = (1.0 - first) * trans[...]
    turned = invert(info * var, work)
    weight = turned.T
    cov = weight * var
    linear = mul(weight, moving)
    small = mul(rows8(h), jnp.concatenate([cov, linear], axis=1))
    offset = small[0:1, 0:size] + mul(rows8(mean), turned)[0:1]
    vector = small[0:1, size : 2 * size]
    info_moved = mul(moving.T, mul(info, linear))
    out[...] = pack(linear, offset, cov, vector, info_moved)


def put_sent(out, sent, core):
    size = out.shape[1]
    sent[...] = out[pl.ds(core * size, size + 8)]


def put_edge(cov, offset, sent):
    size = cov.shape[0]
    part = size // 2
    below, _ = masks(part)
    _, diag = masks(size)
    diagonal = jnp.sum(jnp.where(diag, cov, 0.0), axis=0, keepdims=True)
    sent[0:8] = jnp.concatenate([offset, diagonal, jnp.zeros((6, size), f32)], axis=0)
    shared = jnp.where(below, cov[0:part, 0:part], cov[part:, part:])
    sent[8 : part + 8] = jnp.concatenate([shared, cov[0:part, part:]], axis=1)


def take_edge(ref):
    size = ref.shape[1]
    part = size // 2
    below, _ = masks(part)
    _, diag = masks(size)
    shared = ref[8 : part + 8, 0:part]
    corner = ref[8 : part + 8, part:size]
    turned = shared.T
    cov = jnp.concatenate(
        [
            jnp.concatenate([jnp.where(below, shared, turned), corner], axis=1),
            jnp.concatenate([corner.T, jnp.where(below, turned, shared)], axis=1),
        ],
        axis=0,
    )
    return jnp.where(diag, ref[1:2], cov), ref[0:1]


def pair_kernel(flags, mine, other, state, sent, sides, *work):
    size = mine.shape[1]
    core = flags[1]
    high = core == 1
    own = unpack_whole(mine)
    far = unpack_whole(other)
    whole = pack(*fold(*ordered(high, own, far), work))
    state[...] = whole
    put_sent(state, sent, core)
    _, diag = masks(size)
    eye = diag.astype(f32)
    none = jnp.zeros((8, size), f32)
    neutral = jnp.concatenate([none, eye, jnp.zeros((size, size), f32)], axis=0)
    sides[1] = jnp.where(high, whole, mine[...])
    sides[0] = jnp.where(high, neutral, pack(*dual(jnp.logical_not(high), far)))


def fold_kernel(flags, bits, state, got, far, out, sent, *work):
    core = flags[1]
    high = bits[0] == 1
    received = unpack_halves(got, far, core)
    out[...] = pack(*fold(*ordered(high, unpack_whole(out), received), work))
    put_sent(out, sent, core)


def edge_kernel(flags, bits, state, got, far, sent, *work):
    core = flags[1]
    high = bits[0] == 1
    upper = bits[1] == 1
    first, second = ordered(
        jnp.logical_xor(high, upper), unpack_whole(state), unpack_halves(got, far, core)
    )
    _, offset, cov, _, _ = dual(upper, first)
    cov, offset = half_fold(cov, offset, dual(upper, second), work)
    put_edge(cov, offset, sent)


def side_kernel(flags, bits, sides, got, far, out, *work):
    core = flags[1]
    bit = bits[0]
    received = dual(bit == 0, unpack_halves(got, far, core))
    out[bit] = pack(*fold(received, unpack_whole(out.at[bit]), work))


def two_sides_kernel(flags, bits, sides, got_a, far_a, got_b, far_b, out, received, *work):
    core = flags[1]

    def update(index, carry):
        bit = jnp.where(index == 0, bits[2], bits[0])

        @pl.when(index == 0)
        def _():
            received[...] = pack(*dual(bit == 0, unpack_halves(got_a, far_a, core)))

        @pl.when(index == 1)
        def _():
            received[...] = pack(*dual(bit == 0, unpack_halves(got_b, far_b, core)))

        out[bit] = pack(*fold(unpack_whole(received), unpack_whole(out.at[bit]), work))
        return carry

    lax.fori_loop(0, 2, update, 0)


def close_kernel(flags, bits, sides, got, far, out, one, two, three, *work):
    size = got.shape[1]
    core = flags[1]
    bit = bits[0]
    upper = bits[1] == 1
    _, diag = masks(size)
    one[...] = pack(*dual(bit == 0, unpack_halves(got, far, core)))
    two[...] = sides[bit]

    def turn(index, carry):
        three[...] = pack(*fold(unpack_whole(one), unpack_whole(two), work))

        @pl.when(index == 0)
        def _():
            fresh = unpack_whole(three)
            kept = unpack_whole(sides.at[1 - bit])
            back, front = ordered(bit == 1, fresh, kept)
            eye = diag.astype(f32)
            back_lin, back_off, back_cov, back_vec, back_inf = back
            front_lin, mean, cov, front_vec, front_inf = front
            none = jnp.zeros((1, size), f32)
            zero = jnp.zeros((size, size), f32)
            one[...] = pack(
                jnp.where(upper, front_lin, cov),
                mean,
                cov,
                jnp.where(upper, front_vec, none),
                jnp.where(upper, front_inf, zero),
            )
            two[...] = pack(
                jnp.where(upper, eye, back_lin.T),
                jnp.where(upper, none, -back_vec),
                jnp.where(upper, zero, back_inf),
                back_off,
                back_cov,
            )

        return carry

    lax.fori_loop(0, 2, turn, 0)
    linear, offset, spread, vector, info = unpack_whole(three)
    _, mean, cov, _, _ = unpack_whole(one)
    base = jnp.where(upper, spread, cov - info)
    base = jnp.sum(jnp.where(diag, base, 0.0), axis=0, keepdims=True)
    out[0:8] = jnp.concatenate(
        [
            jnp.where(upper, vector, -offset),
            jnp.where(upper, offset, mean + vector),
            base,
            jnp.zeros((5, size), f32),
        ],
        axis=0,
    )
    out[8 : size + 8] = jnp.where(upper, linear.T, linear)
    out[size + 8 : 2 * size + 8] = jnp.where(upper, info, spread)


def last_kernel(flags, bits, closed, received, mean_out, var_out, work):
    size = received.shape[1]
    sign = (2 * bits[1] - 1).astype(f32)
    matrix, offset = take_edge(received)
    rows = closed[0:8]
    turned = closed[8 : size + 8]
    spread = mul(matrix, turned)
    push = offset + mul(rows8(rows[0:1]), matrix)[0:1]
    weight = invert(mul(matrix, closed[size + 8 : 2 * size + 8]), work)
    moved = mul_nt(rows8(push), weight)
    mean_out[...] = rows[1:2] + mul(moved, turned)[0:1]
    var_out[...] = rows[2:3] + sign * jnp.sum(
        turned * mul(weight, spread), axis=0, keepdims=True
    )


def run(body, out_shapes, size, *args, scalars=0, extra=(), aliases={}):
    vmem = pl.BlockSpec(memory_space=pltpu.VMEM)
    spaces = [
        pl.BlockSpec(memory_space=pltpu.SMEM) if index < scalars else vmem
        for index in range(len(args))
    ]
    single = len(out_shapes) == 1
    shapes = [jax.ShapeDtypeStruct(shape, f32) for shape in out_shapes]
    return pl.pallas_call(
        body,
        out_shape=shapes[0] if single else shapes,
        in_specs=spaces,
        out_specs=vmem if single else [vmem] * len(shapes),
        scratch_shapes=list(extra),
        input_output_aliases=aliases,
        compiler_params=pltpu.CompilerParams(vmem_limit_bytes=16 * 1024 * 1024),
        name=body.__name__,
    )(*args)


def local(
    transition, noise_var, prior_mean, prior_var, obs_op, obs_value, obs_noise, obs_block, obs_count
):
    size = transition.shape[0]
    devices = lax.axis_size("tm")
    levels = (devices - 1).bit_length()
    device = lax.axis_index("tm")
    core = device % 2
    flags = jnp.stack([device, core]).astype(jnp.int32)
    _, slots, stations, width = obs_op.shape
    assert size == 2 * stations
    tall = 2 * slots + 8

    def placed(value, at):
        value = value.astype(f32)
        return jnp.pad(value, ((at, tall - at - value.shape[0]), (0, stations - value.shape[1])))

    rows = (
        placed(obs_value[0], 0)
        + placed(obs_noise[0], slots)
        + placed(noise_var.reshape(2, stations), 2 * slots)
        + placed(prior_mean.reshape(2, stations), 2 * slots + 2)
        + placed(prior_var.reshape(2, stations), 2 * slots + 4)
        + placed(obs_count[:, None], 2 * slots + 6)
        + placed(obs_block, 2 * slots + 7)
    )
    message = (2 * size + 8, size)
    half = (size + 8, size)
    inverse_work = [pltpu.VMEM((2 * size, size), f32)]

    def traded(value, level):
        return lax.ppermute(value, "tm", [(d, d ^ (1 << level)) for d in range(devices)])

    element = run(
        build_kernel,
        [message],
        size,
        flags,
        transition,
        obs_op[0],
        rows,
        scalars=1,
        extra=[pltpu.VMEM((size, size), f32)] + inverse_work,
    )
    other = traded(element, 0)
    state, sent, sides = run(
        pair_kernel,
        [message, half, (2,) + message],
        size,
        flags,
        element,
        other,
        scalars=1,
        extra=inverse_work,
    )
    for level in range(1, levels - 1):
        bits = jnp.stack([(device >> (level + k)) % 2 for k in (0, 1, -1)]).astype(jnp.int32)
        got = traded(sent, level)
        got, sides = lax.optimization_barrier((got, sides))
        far = traded(got, 0)
        now = (flags, bits, state, got, far)
        if level < levels - 2:
            state, sent = run(
                fold_kernel,
                [message, half],
                size,
                *now,
                scalars=2,
                extra=inverse_work,
                aliases={2: 0},
            )
        else:
            sent = run(edge_kernel, [(size // 2 + 8, size)], size, *now, scalars=2, extra=inverse_work)
        _, sides = lax.optimization_barrier((sent, sides))
        now = (flags, bits, sides, got, far)
        if level < levels - 2 and (level > 1 and level % 2 == 0):
            waiting = (got, far)
        elif level < levels - 2 and level > 1:
            sides = run(
                two_sides_kernel,
                [(2,) + message],
                size,
                flags,
                bits,
                sides,
                *waiting,
                got,
                far,
                scalars=2,
                extra=[pltpu.VMEM(message, f32)] + inverse_work,
                aliases={2: 0},
            )
        elif level == 1:
            sides = run(
                side_kernel,
                [(2,) + message],
                size,
                *now,
                scalars=2,
                extra=inverse_work,
                aliases={2: 0},
            )
        else:
            closed = run(
                close_kernel,
                [message],
                size,
                *now,
                scalars=2,
                extra=[pltpu.VMEM(message, f32)] * 3 + inverse_work,
            )
    received = traded(sent, levels - 1)
    mean, var = run(
        last_kernel,
        [(1, size), (1, size)],
        size,
        flags,
        bits,
        closed,
        received,
        scalars=2,
        extra=inverse_work,
    )
    return mean, var


def solution(mesh):
    return jax.shard_map(
        local,
        mesh=mesh,
        in_specs=(
            P(),
            P(),
            P(),
            P(),
            P("tm", None, None, None),
            P("tm", None, None),
            P("tm", None, None),
            P("tm", None),
            P("tm"),
        ),
        out_specs=(P("tm", None), P("tm", None)),
        check_vma=False,
    )
```

profile of v0, /device:TPU:1, one launch (start us, length us, event | category | flops | bytes accessed | tf_op | source)
XLA Modules:
  0.0 130.7 jit_solution(9561338839839192201)
XLA Ops:
  4.7 3.6 %build_kernel.1.mine = f32[520,256]{1,0:T(8,128)S(1)} custom-call(s32[2]{0:T(128)S(1)} %pad_add_fusion.1.flags, f32[256,256]{1,0:T(8,128)S(1)} %copy-done, bf16[8,128,128]{2,1,0:T(8,128)(2,1)S(1)} %bitcast.17, f32[24,128]{1,0:T(8,128)S(1)} %pad_add_fusion.rows), custom_call_target="tpu_custom_call" | custom-call | tf_op jit(solution)/shard_map/build_kernel/pallas_call | solution.py:427
  8.3 3.6 %collective-permute-start = (f32[520,256]{1,0:T(8,128)S(1)}, f32[520,256]{1,0:T(8,128)S(1)}, u32[]{:S(2)}, u32[]{:S(2)}) collective-permute-start(f32[520,256]{1,0:T(8,128)S(1)} %build_kernel.1.mine), channel_id=1, source_target_pairs={{0,1},{1,0},{2,3},{3,2},{4,5},{5,4},{6,7},{7,6},{8,9},{9,8},{10,11... | collective-permute-start | bytes 1597448 | tf_op jit(solution)/shard_map/ppermute | solution.py:470
  11.8 1.5 %collective-permute-done.other = f32[520,256]{1,0:T(8,128)S(1)} collective-permute-done((f32[520,256]{1,0:T(8,128)S(1)}, f32[520,256]{1,0:T(8,128)S(1)}, u32[]{:S(2)}, u32[]{:S(2)}) %collective-permute-start) | collective-permute-done | bytes 532512 | tf_op jit(solution)/shard_map/ppermute | solution.py:470
  13.4 3.8 %pair_kernel.1 = (f32[520,256]{1,0:T(8,128)S(1)}, f32[264,256]{1,0:T(8,128)S(1)}, f32[2,520,256]{2,1,0:T(8,128)S(1)}) custom-call(s32[2]{0:T(128)S(1)} %pad_add_fusion.1.flags, f32[520,256]{1,0:T(8,128)S(1)} %build_kernel.1.mine, f32[520,256]{1,0:T(8,128)S(1)} %collective-permute-done.other), custom_call_target="tpu_custom_call" | custom-call | tf_op jit(solution)/shard_map/pair_kernel/pallas_call | solution.py:427
  17.3 7.7 %collective-permute-done.1.got = f32[264,256]{1,0:T(8,128)S(1)} collective-permute-done((f32[264,256]{1,0:T(8,128)S(1)}, f32[264,256]{1,0:T(8,128)S(1)}, u32[]{:S(2)}, u32[]{:S(2)}) %collective-permute-start.1) | collective-permute-done | bytes 270368 | tf_op jit(solution)/shard_map/ppermute | solution.py:470
  27.4 3.9 %fold_kernel.5 = (f32[520,256]{1,0:T(8,128)S(1)}, f32[264,256]{1,0:T(8,128)S(1)}) custom-call(s32[2]{0:T(128)S(1)} %pad_add_fusion.1.flags, s32[3]{0:T(128)S(1)} %pad_add_fusion.7.bits, f32[520,256]{1,0:T(8,128)S(1)} %get-tuple-element.33.state, f32[264,256]{1,0:T(8,128)S(1)} %collective-permute-done.1.got, ...), custom_call_target="tpu_custom_call", output_to_operand_aliasing={{0}: (2, {})} | custom-call | tf_op jit(solution)/shard_map/fold_kernel/pallas_call | solution.py:427
  31.4 3.2 %side_kernel.1.sides = f32[2,520,256]{2,1,0:T(8,128)S(1)} custom-call(s32[2]{0:T(128)S(1)} %pad_add_fusion.1.flags, s32[3]{0:T(128)S(1)} %pad_add_fusion.7.bits, f32[2,520,256]{2,1,0:T(8,128)S(1)} %get-tuple-element.40.sides, f32[264,256]{1,0:T(8,128)S(1)} %collective-permute-done.1.got, ...), custom_call_target="tpu_custom_call", output_to_operand_aliasing={{}: (2, {})} | custom-call | tf_op jit(solution)/shard_map/side_kernel/pallas_call | solution.py:427
  34.5 6.0 %collective-permute-done.3.got.got_a = f32[264,256]{1,0:T(8,128)S(1)} collective-permute-done((f32[264,256]{1,0:T(8,128)S(1)}, f32[264,256]{1,0:T(8,128)S(1)}, u32[]{:S(2)}, u32[]{:S(2)}) %collective-permute-start.3) | collective-permute-done | bytes 270368 | tf_op jit(solution)/shard_map/ppermute | solution.py:470
  40.5 1.2 collective-permute-start.4
  43.0 4.1 %fold_kernel.6 = (f32[520,256]{1,0:T(8,128)S(1)}, f32[264,256]{1,0:T(8,128)S(1)}) custom-call(s32[2]{0:T(128)S(1)} %pad_add_fusion.1.flags, s32[3]{0:T(128)S(1)} %pad_add_fusion.6.bits, f32[520,256]{1,0:T(8,128)S(1)} %get-tuple-element.37.state, f32[264,256]{1,0:T(8,128)S(1)} %collective-permute-done.3.got.got_a, ...), custom_call_target="tpu_custom_call", output_to_operand_aliasing={{0}: (2, {})} | custom-call | tf_op jit(solution)/shard_map/fold_kernel/pallas_call | solution.py:427
  47.2 7.7 %collective-permute-done.5.got.got_b = f32[264,256]{1,0:T(8,128)S(1)} collective-permute-done((f32[264,256]{1,0:T(8,128)S(1)}, f32[264,256]{1,0:T(8,128)S(1)}, u32[]{:S(2)}, u32[]{:S(2)}) %collective-permute-start.5) | collective-permute-done | bytes 270368 | tf_op jit(solution)/shard_map/ppermute | solution.py:470
  57.2 3.9 %fold_kernel.7 = (f32[520,256]{1,0:T(8,128)S(1)}, f32[264,256]{1,0:T(8,128)S(1)}) custom-call(s32[2]{0:T(128)S(1)} %pad_add_fusion.1.flags, s32[3]{0:T(128)S(1)} %pad_add_fusion.5.bits, f32[520,256]{1,0:T(8,128)S(1)} %get-tuple-element.42.state, f32[264,256]{1,0:T(8,128)S(1)} %collective-permute-done.5.got.got_b, ...), custom_call_target="tpu_custom_call", output_to_operand_aliasing={{0}: (2, {})} | custom-call | tf_op jit(solution)/shard_map/fold_kernel/pallas_call | solution.py:427
  61.2 7.1 %two_sides_kernel.2.sides = f32[2,520,256]{2,1,0:T(8,128)S(1)} custom-call(s32[2]{0:T(128)S(1)} %pad_add_fusion.1.flags, s32[3]{0:T(128)S(1)} %pad_add_fusion.5.bits, f32[2,520,256]{2,1,0:T(8,128)S(1)} %side_kernel.1.sides, f32[264,256]{1,0:T(8,128)S(1)} %collective-permute-done.3.got.got_a, ...), custom_call_target="tpu_custom_call", output_to_operand_aliasing={{}: (2, {})} | custom-call | tf_op jit(solution)/shard_map/two_sides_kernel/pallas_call | solution.py:427
  68.3 2.0 %collective-permute-done.7.got.got_a = f32[264,256]{1,0:T(8,128)S(1)} collective-permute-done((f32[264,256]{1,0:T(8,128)S(1)}, f32[264,256]{1,0:T(8,128)S(1)}, u32[]{:S(2)}, u32[]{:S(2)}) %collective-permute-start.7) | collective-permute-done | bytes 270368 | tf_op jit(solution)/shard_map/ppermute | solution.py:470
  70.4 1.2 collective-permute-start.8
  72.8 4.2 %fold_kernel.8 = (f32[520,256]{1,0:T(8,128)S(1)}, f32[264,256]{1,0:T(8,128)S(1)}) custom-call(s32[2]{0:T(128)S(1)} %pad_add_fusion.1.flags, s32[3]{0:T(128)S(1)} %pad_add_fusion.4.bits, f32[520,256]{1,0:T(8,128)S(1)} %get-tuple-element.47.state, f32[264,256]{1,0:T(8,128)S(1)} %collective-permute-done.7.got.got_a, ...), custom_call_target="tpu_custom_call", output_to_operand_aliasing={{0}: (2, {})} | custom-call | tf_op jit(solution)/shard_map/fold_kernel/pallas_call | solution.py:427
  77.1 7.7 %collective-permute-done.9.got.got_b = f32[264,256]{1,0:T(8,128)S(1)} collective-permute-done((f32[264,256]{1,0:T(8,128)S(1)}, f32[264,256]{1,0:T(8,128)S(1)}, u32[]{:S(2)}, u32[]{:S(2)}) %collective-permute-start.9) | collective-permute-done | bytes 270368 | tf_op jit(solution)/shard_map/ppermute | solution.py:470
  87.1 4.6 %fold_kernel.9 = (f32[520,256]{1,0:T(8,128)S(1)}, f32[264,256]{1,0:T(8,128)S(1)}) custom-call(s32[2]{0:T(128)S(1)} %pad_add_fusion.1.flags, s32[3]{0:T(128)S(1)} %pad_add_fusion.3.bits, f32[520,256]{1,0:T(8,128)S(1)} %get-tuple-element.52.state, f32[264,256]{1,0:T(8,128)S(1)} %collective-permute-done.9.got.got_b, ...), custom_call_target="tpu_custom_call", output_to_operand_aliasing={{0}: (2, {})} | custom-call | tf_op jit(solution)/shard_map/fold_kernel/pallas_call | solution.py:427
  92.4 8.0 %two_sides_kernel.3.sides = f32[2,520,256]{2,1,0:T(8,128)S(1)} custom-call(s32[2]{0:T(128)S(1)} %pad_add_fusion.1.flags, s32[3]{0:T(128)S(1)} %pad_add_fusion.3.bits, f32[2,520,256]{2,1,0:T(8,128)S(1)} %two_sides_kernel.2.sides, f32[264,256]{1,0:T(8,128)S(1)} %collective-permute-done.7.got.got_a, ...), custom_call_target="tpu_custom_call", output_to_operand_aliasing={{}: (2, {})} | custom-call | tf_op jit(solution)/shard_map/two_sides_kernel/pallas_call | solution.py:427
  100.5 6.2 %collective-permute-done.11.got = f32[264,256]{1,0:T(8,128)S(1)} collective-permute-done((f32[264,256]{1,0:T(8,128)S(1)}, f32[264,256]{1,0:T(8,128)S(1)}, u32[]{:S(2)}, u32[]{:S(2)}) %collective-permute-start.11) | collective-permute-done | bytes 270368 | tf_op jit(solution)/shard_map/ppermute | solution.py:470
  108.3 5.0 %edge_kernel.1 = f32[136,256]{1,0:T(8,128)S(1)} custom-call(s32[2]{0:T(128)S(1)} %pad_add_fusion.1.flags, s32[3]{0:T(128)S(1)} %pad_add_fusion.2.bits, f32[520,256]{1,0:T(8,128)S(1)} %get-tuple-element.57.state, f32[264,256]{1,0:T(8,128)S(1)} %collective-permute-done.11.got, f32[264,256]{1,0:T(8,128)S(1)} %collective-permute-done.12.far), custom_call_target="tpu_custom_call" | custom-call | tf_op jit(solution)/shard_map/edge_kernel/pallas_call | solution.py:427
  113.3 4.4 %collective-permute-start.13 = (f32[136,256]{1,0:T(8,128)S(1)}, f32[136,256]{1,0:T(8,128)S(1)}, u32[]{:S(2)}, u32[]{:S(2)}) collective-permute-start(f32[136,256]{1,0:T(8,128)S(1)} %edge_kernel.1), channel_id=1, source_target_pairs={{0,128},{1,129},{2,130},{3,131},{4,132},{5,133},{6,134},{7,135},{8... | collective-permute-start | bytes 417800 | tf_op jit(solution)/shard_map/ppermute | solution.py:470
  117.7 8.6 %close_kernel.1.closed = f32[520,256]{1,0:T(8,128)S(1)} custom-call(s32[2]{0:T(128)S(1)} %pad_add_fusion.1.flags, s32[3]{0:T(128)S(1)} %pad_add_fusion.2.bits, f32[2,520,256]{2,1,0:T(8,128)S(1)} %two_sides_kernel.3.sides, f32[264,256]{1,0:T(8,128)S(1)} %collective-permute-done.11.got, f32[264,256]{1,0:T(8,128)S(1)} %collective-permute-done.12.far), custom_call_target="tpu_custom_call" | custom-call | tf_op jit(solution)/shard_map/close_kernel/pallas_call | solution.py:427
  126.3 4.4 %last_kernel.1 = (f32[1,256]{1,0:T(1,128)}, f32[1,256]{1,0:T(1,128)}) custom-call(s32[2]{0:T(128)S(1)} %pad_add_fusion.1.flags, s32[3]{0:T(128)S(1)} %pad_add_fusion.2.bits, f32[520,256]{1,0:T(8,128)S(1)} %close_kernel.1.closed, f32[136,256]{1,0:T(8,128)S(1)} %collective-permute-done.13.received), custom_call_target="tpu_custom_call" | custom-call | tf_op jit(solution)/shard_map/last_kernel/pallas_call | solution.py:427
  (30 shorter events, 15.7 us)
Async XLA Ops:
  2.8 1.0 copy-start
  3.7 0.9 copy-start.1
  8.3 5.1 %collective-permute-start = (f32[520,256]{1,0:T(8,128)S(1)}, f32[520,256]{1,0:T(8,128)S(1)}, u32[]{:S(2)}, u32[]{:S(2)}) collective-permute-start(f32[520,256]{1,0:T(8,128)S(1)} %build_kernel.1.mine), channel_id=1, source_target_pairs={{0,1},{1,0},{2,3},{3,2},{4,5},{5,4},{6,7},{7,6},{8,9},{9,8},{10,11... | collective-permute-start | bytes 1597448 | tf_op jit(solution)/shard_map/ppermute | solution.py:470
  17.2 7.8 %collective-permute-start.1 = (f32[264,256]{1,0:T(8,128)S(1)}, f32[264,256]{1,0:T(8,128)S(1)}, u32[]{:S(2)}, u32[]{:S(2)}) collective-permute-start(f32[264,256]{1,0:T(8,128)S(1)} %get-tuple-element.34), channel_id=1, source_target_pairs={{0,2},{1,3},{2,0},{3,1},{4,6},{5,7},{6,4},{7,5},{8,10},{9,11},{10,... | collective-permute-start | bytes 811016 | tf_op jit(solution)/shard_map/ppermute | solution.py:470
  25.0 2.4 %collective-permute-start.2 = (f32[264,256]{1,0:T(8,128)S(1)}, f32[264,256]{1,0:T(8,128)S(1)}, u32[]{:S(2)}, u32[]{:S(2)}) collective-permute-start(f32[264,256]{1,0:T(8,128)S(1)} %collective-permute-done.1.got), channel_id=1, source_target_pairs={{0,1},{1,0},{2,3},{3,2},{4,5},{5,4},{6,7},{7,6},{8,9},{9,8},{10,11... | collective-permute-start | bytes 811016 | tf_op jit(solution)/shard_map/ppermute | solution.py:470
  31.3 9.3 %collective-permute-start.3 = (f32[264,256]{1,0:T(8,128)S(1)}, f32[264,256]{1,0:T(8,128)S(1)}, u32[]{:S(2)}, u32[]{:S(2)}) collective-permute-start(f32[264,256]{1,0:T(8,128)S(1)} %get-tuple-element.38), channel_id=1, source_target_pairs={{0,4},{1,5},{2,6},{3,7},{4,0},{5,1},{6,2},{7,3},{8,12},{9,13},{10,... | collective-permute-start | bytes 811016 | tf_op jit(solution)/shard_map/ppermute | solution.py:470
  40.5 2.4 %collective-permute-start.4 = (f32[264,256]{1,0:T(8,128)S(1)}, f32[264,256]{1,0:T(8,128)S(1)}, u32[]{:S(2)}, u32[]{:S(2)}) collective-permute-start(f32[264,256]{1,0:T(8,128)S(1)} %collective-permute-done.3.got.got_a), channel_id=1, source_target_pairs={{0,1},{1,0},{2,3},{3,2},{4,5},{5,4},{6,7},{7,6},{8,9},{9,8},{10,11... | collective-permute-start | bytes 811016 | tf_op jit(solution)/shard_map/ppermute | solution.py:470
  47.1 7.8 %collective-permute-start.5 = (f32[264,256]{1,0:T(8,128)S(1)}, f32[264,256]{1,0:T(8,128)S(1)}, u32[]{:S(2)}, u32[]{:S(2)}) collective-permute-start(f32[264,256]{1,0:T(8,128)S(1)} %get-tuple-element.43), channel_id=1, source_target_pairs={{0,8},{1,9},{2,10},{3,11},{4,12},{5,13},{6,14},{7,15},{8,0},{9,1},... | collective-permute-start | bytes 811016 | tf_op jit(solution)/shard_map/ppermute | solution.py:470
  54.8 2.4 %collective-permute-start.6 = (f32[264,256]{1,0:T(8,128)S(1)}, f32[264,256]{1,0:T(8,128)S(1)}, u32[]{:S(2)}, u32[]{:S(2)}) collective-permute-start(f32[264,256]{1,0:T(8,128)S(1)} %collective-permute-done.5.got.got_b), channel_id=1, source_target_pairs={{0,1},{1,0},{2,3},{3,2},{4,5},{5,4},{6,7},{7,6},{8,9},{9,8},{10,11... | collective-permute-start | bytes 811016 | tf_op jit(solution)/shard_map/ppermute | solution.py:470
  61.1 9.2 %collective-permute-start.7 = (f32[264,256]{1,0:T(8,128)S(1)}, f32[264,256]{1,0:T(8,128)S(1)}, u32[]{:S(2)}, u32[]{:S(2)}) collective-permute-start(f32[264,256]{1,0:T(8,128)S(1)} %get-tuple-element.48), channel_id=1, source_target_pairs={{0,16},{1,17},{2,18},{3,19},{4,20},{5,21},{6,22},{7,23},{8,24},{9,... | collective-permute-start | bytes 811016 | tf_op jit(solution)/shard_map/ppermute | solution.py:470
  70.4 2.4 %collective-permute-start.8 = (f32[264,256]{1,0:T(8,128)S(1)}, f32[264,256]{1,0:T(8,128)S(1)}, u32[]{:S(2)}, u32[]{:S(2)}) collective-permute-start(f32[264,256]{1,0:T(8,128)S(1)} %collective-permute-done.7.got.got_a), channel_id=1, source_target_pairs={{0,1},{1,0},{2,3},{3,2},{4,5},{5,4},{6,7},{7,6},{8,9},{9,8},{10,11... | collective-permute-start | bytes 811016 | tf_op jit(solution)/shard_map/ppermute | solution.py:470
  77.0 7.8 %collective-permute-start.9 = (f32[264,256]{1,0:T(8,128)S(1)}, f32[264,256]{1,0:T(8,128)S(1)}, u32[]{:S(2)}, u32[]{:S(2)}) collective-permute-start(f32[264,256]{1,0:T(8,128)S(1)} %get-tuple-element.53), channel_id=1, source_target_pairs={{0,32},{1,33},{2,34},{3,35},{4,36},{5,37},{6,38},{7,39},{8,40},{9,... | collective-permute-start | bytes 811016 | tf_op jit(solution)/shard_map/ppermute | solution.py:470
  84.7 2.4 %collective-permute-start.10 = (f32[264,256]{1,0:T(8,128)S(1)}, f32[264,256]{1,0:T(8,128)S(1)}, u32[]{:S(2)}, u32[]{:S(2)}) collective-permute-start(f32[264,256]{1,0:T(8,128)S(1)} %collective-permute-done.9.got.got_b), channel_id=1, source_target_pairs={{0,1},{1,0},{2,3},{3,2},{4,5},{5,4},{6,7},{7,6},{8,9},{9,8},{10,11... | collective-permute-start | bytes 811016 | tf_op jit(solution)/shard_map/ppermute | solution.py:470
  91.8 14.9 %collective-permute-start.11 = (f32[264,256]{1,0:T(8,128)S(1)}, f32[264,256]{1,0:T(8,128)S(1)}, u32[]{:S(2)}, u32[]{:S(2)}) collective-permute-start(f32[264,256]{1,0:T(8,128)S(1)} %get-tuple-element.58), channel_id=1, source_target_pairs={{0,64},{1,65},{2,66},{3,67},{4,68},{5,69},{6,70},{7,71},{8,72},{9,... | collective-permute-start | bytes 811016 | tf_op jit(solution)/shard_map/ppermute | solution.py:470
  106.7 1.7 %collective-permute-start.12 = (f32[264,256]{1,0:T(8,128)S(1)}, f32[264,256]{1,0:T(8,128)S(1)}, u32[]{:S(2)}, u32[]{:S(2)}) collective-permute-start(f32[264,256]{1,0:T(8,128)S(1)} %collective-permute-done.11.got), channel_id=1, source_target_pairs={{0,1},{1,0},{2,3},{3,2},{4,5},{5,4},{6,7},{7,6},{8,9},{9,8},{10,11... | collective-permute-start | bytes 811016 | tf_op jit(solution)/shard_map/ppermute | solution.py:470
  113.3 13.0 %collective-permute-start.13 = (f32[136,256]{1,0:T(8,128)S(1)}, f32[136,256]{1,0:T(8,128)S(1)}, u32[]{:S(2)}, u32[]{:S(2)}) collective-permute-start(f32[136,256]{1,0:T(8,128)S(1)} %edge_kernel.1), channel_id=1, source_target_pairs={{0,128},{1,129},{2,130},{3,131},{4,132},{5,133},{6,134},{7,135},{8... | collective-permute-start | bytes 417800 | tf_op jit(solution)/shard_map/ppermute | solution.py:470
where the time goes:
time: 131 us
  Pallas kernels  64.3 us (49%)
  waiting for transfers between devices  45.4 us (35%)
  starting transfers between devices  15.7 us (12%)
  other arithmetic  1.95 us (1%)
  local copies, waits for them, and re-layouts  1.89 us (1%)
  between operations  1.44 us (1%)
    pallas_call x13, Pallas kernels, run(): pl.pallas_call(body, out_shape=shapes[0] if single else shapes, in_specs=...  64.3 us
    ppermute x14, waiting for transfers between devices, traded(): lax.ppermute(value, 'tm', [(d, d ^ 1 << level) for d in range(devices)])  45.4 us
    ppermute x14, starting transfers between devices, traded(): lax.ppermute(value, 'tm', [(d, d ^ 1 << level) for d in range(devices)])  15.7 us
  transfers between devices with their start and end apart: 14, of which 13 were waited for; matrix products, arithmetic and copies ran while one was open for 0% of the time, Pallas kernels for 21%

commit v1 on v0

--- a/solution.py
+++ b/solution.py
@@ -56,7 +56,7 @@
     _, diag = masks(size)
     eye = diag.astype(f32)
     magnitude = jnp.abs(m)
-    bound = jnp.max(jnp.sum(magnitude, axis=0, keepdims=True))
+    bound = jnp.max(jnp.sum(magnitude, axis=1, keepdims=True))
     scale = 2.0 / (2.0 + bound)
     work[0:size] = scale * eye
     work[size : 2 * size] = (1.0 - scale) * eye - scale * m
@@ -511,9 +511,9 @@
             sent = run(edge_kernel, [(size // 2 + 8, size)], size, *now, scalars=2, extra=inverse_work)
         _, sides = lax.optimization_barrier((sent, sides))
         now = (flags, bits, sides, got, far)
-        if level < levels - 2 and (level > 1 and level % 2 == 0):
+        if level % 2 == 1 and level < levels - 3:
             waiting = (got, far)
-        elif level < levels - 2 and level > 1:
+        elif level % 2 == 0 and level < levels - 2:
             sides = run(
                 two_sides_kernel,
                 [(2,) + message],
@@ -528,7 +528,7 @@
                 extra=[pltpu.VMEM(message, f32)] + inverse_work,
                 aliases={2: 0},
             )
-        elif level == 1:
+        elif level < levels - 2:
             sides = run(
                 side_kernel,
                 [(2,) + message],

time: 131 us -> 131 us (level)
  no operation moved by 1% of the time
where the time goes in v1:
time: 131 us
  Pallas kernels  64.3 us (49%)
  waiting for transfers between devices  45.3 us (35%)
  starting transfers between devices  15.9 us (12%)
  other arithmetic  1.95 us (1%)
  local copies, waits for them, and re-layouts  1.89 us (1%)
  between operations  1.44 us (1%)
    pallas_call x13, Pallas kernels, run(): pl.pallas_call(body, out_shape=shapes[0] if single else shapes, in_specs=...  64.3 us
    ppermute x14, waiting for transfers between devices, traded(): lax.ppermute(value, 'tm', [(d, d ^ 1 << level) for d in range(devices)])  45.3 us
    ppermute x14, starting transfers between devices, traded(): lax.ppermute(value, 'tm', [(d, d ^ 1 << level) for d in range(devices)])  15.9 us
  transfers between devices with their start and end apart: 14, of which 13 were waited for; matrix products, arithmetic and copies ran while one was open for 0% of the time, Pallas kernels for 21%

profile of v1, /device:TPU:1, one launch (start us, length us, event | category | flops | bytes accessed | tf_op | source)
XLA Modules:
  0.0 130.7 jit_solution(4349242751826360418)
XLA Ops:
  4.7 3.4 %build_kernel.1.mine = f32[520,256]{1,0:T(8,128)S(1)} custom-call(s32[2]{0:T(128)S(1)} %pad_add_fusion.1.flags, f32[256,256]{1,0:T(8,128)S(1)} %copy-done, bf16[8,128,128]{2,1,0:T(8,128)(2,1)S(1)} %bitcast.17, f32[24,128]{1,0:T(8,128)S(1)} %pad_add_fusion.rows), custom_call_target="tpu_custom_call" | custom-call | tf_op jit(solution)/shard_map/build_kernel/pallas_call | solution.py:427
  8.1 3.8 %collective-permute-start = (f32[520,256]{1,0:T(8,128)S(1)}, f32[520,256]{1,0:T(8,128)S(1)}, u32[]{:S(2)}, u32[]{:S(2)}) collective-permute-start(f32[520,256]{1,0:T(8,128)S(1)} %build_kernel.1.mine), channel_id=1, source_target_pairs={{0,1},{1,0},{2,3},{3,2},{4,5},{5,4},{6,7},{7,6},{8,9},{9,8},{10,11... | collective-permute-start | bytes 1597448 | tf_op jit(solution)/shard_map/ppermute | solution.py:470
  11.9 1.5 %collective-permute-done.other = f32[520,256]{1,0:T(8,128)S(1)} collective-permute-done((f32[520,256]{1,0:T(8,128)S(1)}, f32[520,256]{1,0:T(8,128)S(1)}, u32[]{:S(2)}, u32[]{:S(2)}) %collective-permute-start) | collective-permute-done | bytes 532512 | tf_op jit(solution)/shard_map/ppermute | solution.py:470
  13.5 3.8 %pair_kernel.1 = (f32[520,256]{1,0:T(8,128)S(1)}, f32[264,256]{1,0:T(8,128)S(1)}, f32[2,520,256]{2,1,0:T(8,128)S(1)}) custom-call(s32[2]{0:T(128)S(1)} %pad_add_fusion.1.flags, f32[520,256]{1,0:T(8,128)S(1)} %build_kernel.1.mine, f32[520,256]{1,0:T(8,128)S(1)} %collective-permute-done.other), custom_call_target="tpu_custom_call" | custom-call | tf_op jit(solution)/shard_map/pair_kernel/pallas_call | solution.py:427
  17.4 7.7 %collective-permute-done.1.got.got_a = f32[264,256]{1,0:T(8,128)S(1)} collective-permute-done((f32[264,256]{1,0:T(8,128)S(1)}, f32[264,256]{1,0:T(8,128)S(1)}, u32[]{:S(2)}, u32[]{:S(2)}) %collective-permute-start.1) | collective-permute-done | bytes 270368 | tf_op jit(solution)/shard_map/ppermute | solution.py:470
  27.4 3.9 %fold_kernel.5 = (f32[520,256]{1,0:T(8,128)S(1)}, f32[264,256]{1,0:T(8,128)S(1)}) custom-call(s32[2]{0:T(128)S(1)} %pad_add_fusion.1.flags, s32[3]{0:T(128)S(1)} %pad_add_fusion.7.bits, f32[520,256]{1,0:T(8,128)S(1)} %get-tuple-element.33.state, f32[264,256]{1,0:T(8,128)S(1)} %collective-permute-done.1.got.got_a, ...), custom_call_target="tpu_custom_call", output_to_operand_aliasing={{0}: (2, {})} | custom-call | tf_op jit(solution)/shard_map/fold_kernel/pallas_call | solution.py:427
  31.5 9.2 %collective-permute-done.3.got.got_b = f32[264,256]{1,0:T(8,128)S(1)} collective-permute-done((f32[264,256]{1,0:T(8,128)S(1)}, f32[264,256]{1,0:T(8,128)S(1)}, u32[]{:S(2)}, u32[]{:S(2)}) %collective-permute-start.3) | collective-permute-done | bytes 270368 | tf_op jit(solution)/shard_map/ppermute | solution.py:470
  43.0 3.9 %fold_kernel.6 = (f32[520,256]{1,0:T(8,128)S(1)}, f32[264,256]{1,0:T(8,128)S(1)}) custom-call(s32[2]{0:T(128)S(1)} %pad_add_fusion.1.flags, s32[3]{0:T(128)S(1)} %pad_add_fusion.6.bits, f32[520,256]{1,0:T(8,128)S(1)} %get-tuple-element.37.state, f32[264,256]{1,0:T(8,128)S(1)} %collective-permute-done.3.got.got_b, ...), custom_call_target="tpu_custom_call", output_to_operand_aliasing={{0}: (2, {})} | custom-call | tf_op jit(solution)/shard_map/fold_kernel/pallas_call | solution.py:427
  47.2 6.4 %two_sides_kernel.2.sides = f32[2,520,256]{2,1,0:T(8,128)S(1)} custom-call(s32[2]{0:T(128)S(1)} %pad_add_fusion.1.flags, s32[3]{0:T(128)S(1)} %pad_add_fusion.6.bits, f32[2,520,256]{2,1,0:T(8,128)S(1)} %get-tuple-element.45.sides, f32[264,256]{1,0:T(8,128)S(1)} %collective-permute-done.1.got.got_a, ...), custom_call_target="tpu_custom_call", output_to_operand_aliasing={{}: (2, {})} | custom-call | tf_op jit(solution)/shard_map/two_sides_kernel/pallas_call | solution.py:427
  53.6 1.3 collective-permute-done.5.got.got_a
  54.9 1.2 collective-permute-start.6
  57.3 3.9 %fold_kernel.7 = (f32[520,256]{1,0:T(8,128)S(1)}, f32[264,256]{1,0:T(8,128)S(1)}) custom-call(s32[2]{0:T(128)S(1)} %pad_add_fusion.1.flags, s32[3]{0:T(128)S(1)} %pad_add_fusion.5.bits, f32[520,256]{1,0:T(8,128)S(1)} %get-tuple-element.42.state, f32[264,256]{1,0:T(8,128)S(1)} %collective-permute-done.5.got.got_a, ...), custom_call_target="tpu_custom_call", output_to_operand_aliasing={{0}: (2, {})} | custom-call | tf_op jit(solution)/shard_map/fold_kernel/pallas_call | solution.py:427
  61.3 9.2 %collective-permute-done.7.got.got_b = f32[264,256]{1,0:T(8,128)S(1)} collective-permute-done((f32[264,256]{1,0:T(8,128)S(1)}, f32[264,256]{1,0:T(8,128)S(1)}, u32[]{:S(2)}, u32[]{:S(2)}) %collective-permute-start.7) | collective-permute-done | bytes 270368 | tf_op jit(solution)/shard_map/ppermute | solution.py:470
  70.4 1.2 collective-permute-start.8
  72.9 4.1 %fold_kernel.8 = (f32[520,256]{1,0:T(8,128)S(1)}, f32[264,256]{1,0:T(8,128)S(1)}) custom-call(s32[2]{0:T(128)S(1)} %pad_add_fusion.1.flags, s32[3]{0:T(128)S(1)} %pad_add_fusion.4.bits, f32[520,256]{1,0:T(8,128)S(1)} %get-tuple-element.47.state, f32[264,256]{1,0:T(8,128)S(1)} %collective-permute-done.7.got.got_b, ...), custom_call_target="tpu_custom_call", output_to_operand_aliasing={{0}: (2, {})} | custom-call | tf_op jit(solution)/shard_map/fold_kernel/pallas_call | solution.py:427
  77.1 7.3 %two_sides_kernel.3.sides = f32[2,520,256]{2,1,0:T(8,128)S(1)} custom-call(s32[2]{0:T(128)S(1)} %pad_add_fusion.1.flags, s32[3]{0:T(128)S(1)} %pad_add_fusion.4.bits, f32[2,520,256]{2,1,0:T(8,128)S(1)} %two_sides_kernel.2.sides, f32[264,256]{1,0:T(8,128)S(1)} %collective-permute-done.5.got.got_a, ...), custom_call_target="tpu_custom_call", output_to_operand_aliasing={{}: (2, {})} | custom-call | tf_op jit(solution)/shard_map/two_sides_kernel/pallas_call | solution.py:427
  84.8 1.2 collective-permute-start.10
  87.2 4.4 %fold_kernel.9 = (f32[520,256]{1,0:T(8,128)S(1)}, f32[264,256]{1,0:T(8,128)S(1)}) custom-call(s32[2]{0:T(128)S(1)} %pad_add_fusion.1.flags, s32[3]{0:T(128)S(1)} %pad_add_fusion.3.bits, f32[520,256]{1,0:T(8,128)S(1)} %get-tuple-element.52.state, f32[264,256]{1,0:T(8,128)S(1)} %collective-permute-done.9.got, ...), custom_call_target="tpu_custom_call", output_to_operand_aliasing={{0}: (2, {})} | custom-call | tf_op jit(solution)/shard_map/fold_kernel/pallas_call | solution.py:427
  92.2 4.4 %side_kernel.1.sides = f32[2,520,256]{2,1,0:T(8,128)S(1)} custom-call(s32[2]{0:T(128)S(1)} %pad_add_fusion.1.flags, s32[3]{0:T(128)S(1)} %pad_add_fusion.3.bits, f32[2,520,256]{2,1,0:T(8,128)S(1)} %two_sides_kernel.3.sides, f32[264,256]{1,0:T(8,128)S(1)} %collective-permute-done.9.got, ...), custom_call_target="tpu_custom_call", output_to_operand_aliasing={{}: (2, {})} | custom-call | tf_op jit(solution)/shard_map/side_kernel/pallas_call | solution.py:427
  96.6 9.6 %collective-permute-done.11.got = f32[264,256]{1,0:T(8,128)S(1)} collective-permute-done((f32[264,256]{1,0:T(8,128)S(1)}, f32[264,256]{1,0:T(8,128)S(1)}, u32[]{:S(2)}, u32[]{:S(2)}) %collective-permute-start.11) | collective-permute-done | bytes 270368 | tf_op jit(solution)/shard_map/ppermute | solution.py:470
  108.4 4.9 %edge_kernel.1 = f32[136,256]{1,0:T(8,128)S(1)} custom-call(s32[2]{0:T(128)S(1)} %pad_add_fusion.1.flags, s32[3]{0:T(128)S(1)} %pad_add_fusion.2.bits, f32[520,256]{1,0:T(8,128)S(1)} %get-tuple-element.57.state, f32[264,256]{1,0:T(8,128)S(1)} %collective-permute-done.11.got, f32[264,256]{1,0:T(8,128)S(1)} %collective-permute-done.12.far), custom_call_target="tpu_custom_call" | custom-call | tf_op jit(solution)/shard_map/edge_kernel/pallas_call | solution.py:427
  113.3 3.6 %collective-permute-start.13 = (f32[136,256]{1,0:T(8,128)S(1)}, f32[136,256]{1,0:T(8,128)S(1)}, u32[]{:S(2)}, u32[]{:S(2)}) collective-permute-start(f32[136,256]{1,0:T(8,128)S(1)} %edge_kernel.1), channel_id=1, source_target_pairs={{0,128},{1,129},{2,130},{3,131},{4,132},{5,133},{6,134},{7,135},{8... | collective-permute-start | bytes 417800 | tf_op jit(solution)/shard_map/ppermute | solution.py:470
  116.9 9.4 %close_kernel.1.closed = f32[520,256]{1,0:T(8,128)S(1)} custom-call(s32[2]{0:T(128)S(1)} %pad_add_fusion.1.flags, s32[3]{0:T(128)S(1)} %pad_add_fusion.2.bits, f32[2,520,256]{2,1,0:T(8,128)S(1)} %side_kernel.1.sides, f32[264,256]{1,0:T(8,128)S(1)} %collective-permute-done.11.got, f32[264,256]{1,0:T(8,128)S(1)} %collective-permute-done.12.far), custom_call_target="tpu_custom_call" | custom-call | tf_op jit(solution)/shard_map/close_kernel/pallas_call | solution.py:427
  126.4 4.4 %last_kernel.1 = (f32[1,256]{1,0:T(1,128)}, f32[1,256]{1,0:T(1,128)}) custom-call(s32[2]{0:T(128)S(1)} %pad_add_fusion.1.flags, s32[3]{0:T(128)S(1)} %pad_add_fusion.2.bits, f32[520,256]{1,0:T(8,128)S(1)} %close_kernel.1.closed, f32[136,256]{1,0:T(8,128)S(1)} %collective-permute-done.13.received), custom_call_target="tpu_custom_call" | custom-call | tf_op jit(solution)/shard_map/last_kernel/pallas_call | solution.py:427
  (30 shorter events, 15.5 us)
Async XLA Ops:
  2.8 1.0 copy-start
  3.7 0.9 copy-start.1
  8.1 5.4 %collective-permute-start = (f32[520,256]{1,0:T(8,128)S(1)}, f32[520,256]{1,0:T(8,128)S(1)}, u32[]{:S(2)}, u32[]{:S(2)}) collective-permute-start(f32[520,256]{1,0:T(8,128)S(1)} %build_kernel.1.mine), channel_id=1, source_target_pairs={{0,1},{1,0},{2,3},{3,2},{4,5},{5,4},{6,7},{7,6},{8,9},{9,8},{10,11... | collective-permute-start | bytes 1597448 | tf_op jit(solution)/shard_map/ppermute | solution.py:470
  17.3 7.8 %collective-permute-start.1 = (f32[264,256]{1,0:T(8,128)S(1)}, f32[264,256]{1,0:T(8,128)S(1)}, u32[]{:S(2)}, u32[]{:S(2)}) collective-permute-start(f32[264,256]{1,0:T(8,128)S(1)} %get-tuple-element.34), channel_id=1, source_target_pairs={{0,2},{1,3},{2,0},{3,1},{4,6},{5,7},{6,4},{7,5},{8,10},{9,11},{10,... | collective-permute-start | bytes 811016 | tf_op jit(solution)/shard_map/ppermute | solution.py:470
  25.1 2.4 %collective-permute-start.2 = (f32[264,256]{1,0:T(8,128)S(1)}, f32[264,256]{1,0:T(8,128)S(1)}, u32[]{:S(2)}, u32[]{:S(2)}) collective-permute-start(f32[264,256]{1,0:T(8,128)S(1)} %collective-permute-done.1.got.got_a), channel_id=1, source_target_pairs={{0,1},{1,0},{2,3},{3,2},{4,5},{5,4},{6,7},{7,6},{8,9},{9,8},{10,11... | collective-permute-start | bytes 811016 | tf_op jit(solution)/shard_map/ppermute | solution.py:470
  31.4 9.3 %collective-permute-start.3 = (f32[264,256]{1,0:T(8,128)S(1)}, f32[264,256]{1,0:T(8,128)S(1)}, u32[]{:S(2)}, u32[]{:S(2)}) collective-permute-start(f32[264,256]{1,0:T(8,128)S(1)} %get-tuple-element.38), channel_id=1, source_target_pairs={{0,4},{1,5},{2,6},{3,7},{4,0},{5,1},{6,2},{7,3},{8,12},{9,13},{10,... | collective-permute-start | bytes 811016 | tf_op jit(solution)/shard_map/ppermute | solution.py:470
  40.6 2.4 %collective-permute-start.4 = (f32[264,256]{1,0:T(8,128)S(1)}, f32[264,256]{1,0:T(8,128)S(1)}, u32[]{:S(2)}, u32[]{:S(2)}) collective-permute-start(f32[264,256]{1,0:T(8,128)S(1)} %collective-permute-done.3.got.got_b), channel_id=1, source_target_pairs={{0,1},{1,0},{2,3},{3,2},{4,5},{5,4},{6,7},{7,6},{8,9},{9,8},{10,11... | collective-permute-start | bytes 811016 | tf_op jit(solution)/shard_map/ppermute | solution.py:470
  46.9 7.9 %collective-permute-start.5 = (f32[264,256]{1,0:T(8,128)S(1)}, f32[264,256]{1,0:T(8,128)S(1)}, u32[]{:S(2)}, u32[]{:S(2)}) collective-permute-start(f32[264,256]{1,0:T(8,128)S(1)} %get-tuple-element.43), channel_id=1, source_target_pairs={{0,8},{1,9},{2,10},{3,11},{4,12},{5,13},{6,14},{7,15},{8,0},{9,1},... | collective-permute-start | bytes 811016 | tf_op jit(solution)/shard_map/ppermute | solution.py:470
  54.9 2.4 %collective-permute-start.6 = (f32[264,256]{1,0:T(8,128)S(1)}, f32[264,256]{1,0:T(8,128)S(1)}, u32[]{:S(2)}, u32[]{:S(2)}) collective-permute-start(f32[264,256]{1,0:T(8,128)S(1)} %collective-permute-done.5.got.got_a), channel_id=1, source_target_pairs={{0,1},{1,0},{2,3},{3,2},{4,5},{5,4},{6,7},{7,6},{8,9},{9,8},{10,11... | collective-permute-start | bytes 811016 | tf_op jit(solution)/shard_map/ppermute | solution.py:470
  61.2 9.3 %collective-permute-start.7 = (f32[264,256]{1,0:T(8,128)S(1)}, f32[264,256]{1,0:T(8,128)S(1)}, u32[]{:S(2)}, u32[]{:S(2)}) collective-permute-start(f32[264,256]{1,0:T(8,128)S(1)} %get-tuple-element.48), channel_id=1, source_target_pairs={{0,16},{1,17},{2,18},{3,19},{4,20},{5,21},{6,22},{7,23},{8,24},{9,... | collective-permute-start | bytes 811016 | tf_op jit(solution)/shard_map/ppermute | solution.py:470
  70.4 2.4 %collective-permute-start.8 = (f32[264,256]{1,0:T(8,128)S(1)}, f32[264,256]{1,0:T(8,128)S(1)}, u32[]{:S(2)}, u32[]{:S(2)}) collective-permute-start(f32[264,256]{1,0:T(8,128)S(1)} %collective-permute-done.7.got.got_b), channel_id=1, source_target_pairs={{0,1},{1,0},{2,3},{3,2},{4,5},{5,4},{6,7},{7,6},{8,9},{9,8},{10,11... | collective-permute-start | bytes 811016 | tf_op jit(solution)/shard_map/ppermute | solution.py:470
  77.0 7.8 %collective-permute-start.9 = (f32[264,256]{1,0:T(8,128)S(1)}, f32[264,256]{1,0:T(8,128)S(1)}, u32[]{:S(2)}, u32[]{:S(2)}) collective-permute-start(f32[264,256]{1,0:T(8,128)S(1)} %get-tuple-element.53), channel_id=1, source_target_pairs={{0,32},{1,33},{2,34},{3,35},{4,36},{5,37},{6,38},{7,39},{8,40},{9,... | collective-permute-start | bytes 811016 | tf_op jit(solution)/shard_map/ppermute | solution.py:470
  84.8 2.4 %collective-permute-start.10 = (f32[264,256]{1,0:T(8,128)S(1)}, f32[264,256]{1,0:T(8,128)S(1)}, u32[]{:S(2)}, u32[]{:S(2)}) collective-permute-start(f32[264,256]{1,0:T(8,128)S(1)} %collective-permute-done.9.got), channel_id=1, source_target_pairs={{0,1},{1,0},{2,3},{3,2},{4,5},{5,4},{6,7},{7,6},{8,9},{9,8},{10,11... | collective-permute-start | bytes 811016 | tf_op jit(solution)/shard_map/ppermute | solution.py:470
  91.5 14.6 %collective-permute-start.11 = (f32[264,256]{1,0:T(8,128)S(1)}, f32[264,256]{1,0:T(8,128)S(1)}, u32[]{:S(2)}, u32[]{:S(2)}) collective-permute-start(f32[264,256]{1,0:T(8,128)S(1)} %get-tuple-element.58), channel_id=1, source_target_pairs={{0,64},{1,65},{2,66},{3,67},{4,68},{5,69},{6,70},{7,71},{8,72},{9,... | collective-permute-start | bytes 811016 | tf_op jit(solution)/shard_map/ppermute | solution.py:470
  106.1 2.3 %collective-permute-start.12 = (f32[264,256]{1,0:T(8,128)S(1)}, f32[264,256]{1,0:T(8,128)S(1)}, u32[]{:S(2)}, u32[]{:S(2)}) collective-permute-start(f32[264,256]{1,0:T(8,128)S(1)} %collective-permute-done.11.got), channel_id=1, source_target_pairs={{0,1},{1,0},{2,3},{3,2},{4,5},{5,4},{6,7},{7,6},{8,9},{9,8},{10,11... | collective-permute-start | bytes 811016 | tf_op jit(solution)/shard_map/ppermute | solution.py:470
  113.3 13.0 %collective-permute-start.13 = (f32[136,256]{1,0:T(8,128)S(1)}, f32[136,256]{1,0:T(8,128)S(1)}, u32[]{:S(2)}, u32[]{:S(2)}) collective-permute-start(f32[136,256]{1,0:T(8,128)S(1)} %edge_kernel.1), channel_id=1, source_target_pairs={{0,128},{1,129},{2,130},{3,131},{4,132},{5,133},{6,134},{7,135},{8... | collective-permute-start | bytes 417800 | tf_op jit(solution)/shard_map/ppermute | solution.py:470

commit v2 on v1

--- a/solution.py
+++ b/solution.py
@@ -82,13 +82,13 @@
         return square / (2.0 - square)
 
     lax.while_loop(
-        lambda radius: radius > 2e-2, step, jnp.minimum(bound / (2.0 + bound), 1.0 - 1e-6)
+        lambda radius: radius > 1e-2, step, jnp.minimum(bound / (2.0 + bound), 1.0 - 1e-6)
     )
     split = halves(m)
 
     def more(carry):
         square_of, count = carry
-        return jnp.logical_and(square_of > 2e-3, count < 60)
+        return jnp.logical_and(square_of > 5e-3, count < 60)
 
     def correct(carry):
         _, count = carry

time: 131 us -> 131 us (level)
  starting transfers between devices: 15.9 us -> 18.1 us
  Pallas kernels: 64.3 us -> 62.9 us
    ppermute x14, starting transfers between devices: 15.9 us -> 18.1 us  [traded(): lax.ppermute(value, 'tm', [(d, d ^ 1 << level) for d in range(devices)])]
    pallas_call x13, Pallas kernels: 64.3 us -> 62.9 us  [run(): pl.pallas_call(body, out_shape=shapes[0] if single else shapes, in_specs=...]
where the time goes in v2:
time: 131 us; the launch traced here: 130 us
  Pallas kernels  62.9 us (48%)
  waiting for transfers between devices  44.3 us (34%)
  starting transfers between devices  18.1 us (14%)
  other arithmetic  1.95 us (1%)
  local copies, waits for them, and re-layouts  1.89 us (1%)
  between operations  1.43 us (1%)
    pallas_call x13, Pallas kernels, run(): pl.pallas_call(body, out_shape=shapes[0] if single else shapes, in_specs=...  62.9 us
    ppermute x14, waiting for transfers between devices, traded(): lax.ppermute(value, 'tm', [(d, d ^ 1 << level) for d in range(devices)])  44.3 us
    ppermute x14, starting transfers between devices, traded(): lax.ppermute(value, 'tm', [(d, d ^ 1 << level) for d in range(devices)])  18.1 us
  transfers between devices with their start and end apart: 14, of which 13 were waited for; matrix products, arithmetic and copies ran while one was open for 0% of the time, Pallas kernels for 21%

profile of v2, /device:TPU:1, one launch (start us, length us, event | category | flops | bytes accessed | tf_op | source)
XLA Modules:
  0.0 130.5 jit_solution(3478254366597121577)
XLA Ops:
  4.7 3.6 %build_kernel.1.mine = f32[520,256]{1,0:T(8,128)S(1)} custom-call(s32[2]{0:T(128)S(1)} %pad_add_fusion.1.flags, f32[256,256]{1,0:T(8,128)S(1)} %copy-done, bf16[8,128,128]{2,1,0:T(8,128)(2,1)S(1)} %bitcast.17, f32[24,128]{1,0:T(8,128)S(1)} %pad_add_fusion.rows), custom_call_target="tpu_custom_call" | custom-call | tf_op jit(solution)/shard_map/build_kernel/pallas_call | solution.py:427
  8.3 3.6 %collective-permute-start = (f32[520,256]{1,0:T(8,128)S(1)}, f32[520,256]{1,0:T(8,128)S(1)}, u32[]{:S(2)}, u32[]{:S(2)}) collective-permute-start(f32[520,256]{1,0:T(8,128)S(1)} %build_kernel.1.mine), channel_id=1, source_target_pairs={{0,1},{1,0},{2,3},{3,2},{4,5},{5,4},{6,7},{7,6},{8,9},{9,8},{10,11... | collective-permute-start | bytes 1597448 | tf_op jit(solution)/shard_map/ppermute | solution.py:470
  11.9 1.5 %collective-permute-done.other = f32[520,256]{1,0:T(8,128)S(1)} collective-permute-done((f32[520,256]{1,0:T(8,128)S(1)}, f32[520,256]{1,0:T(8,128)S(1)}, u32[]{:S(2)}, u32[]{:S(2)}) %collective-permute-start) | collective-permute-done | bytes 532512 | tf_op jit(solution)/shard_map/ppermute | solution.py:470
  13.5 3.8 %pair_kernel.1 = (f32[520,256]{1,0:T(8,128)S(1)}, f32[264,256]{1,0:T(8,128)S(1)}, f32[2,520,256]{2,1,0:T(8,128)S(1)}) custom-call(s32[2]{0:T(128)S(1)} %pad_add_fusion.1.flags, f32[520,256]{1,0:T(8,128)S(1)} %build_kernel.1.mine, f32[520,256]{1,0:T(8,128)S(1)} %collective-permute-done.other), custom_call_target="tpu_custom_call" | custom-call | tf_op jit(solution)/shard_map/pair_kernel/pallas_call | solution.py:427
  17.4 7.7 %collective-permute-done.1.got.got_a = f32[264,256]{1,0:T(8,128)S(1)} collective-permute-done((f32[264,256]{1,0:T(8,128)S(1)}, f32[264,256]{1,0:T(8,128)S(1)}, u32[]{:S(2)}, u32[]{:S(2)}) %collective-permute-start.1) | collective-permute-done | bytes 270368 | tf_op jit(solution)/shard_map/ppermute | solution.py:470
  27.4 3.7 %fold_kernel.5 = (f32[520,256]{1,0:T(8,128)S(1)}, f32[264,256]{1,0:T(8,128)S(1)}) custom-call(s32[2]{0:T(128)S(1)} %pad_add_fusion.1.flags, s32[3]{0:T(128)S(1)} %pad_add_fusion.7.bits, f32[520,256]{1,0:T(8,128)S(1)} %get-tuple-element.33.state, f32[264,256]{1,0:T(8,128)S(1)} %collective-permute-done.1.got.got_a, ...), custom_call_target="tpu_custom_call", output_to_operand_aliasing={{0}: (2, {})} | custom-call | tf_op jit(solution)/shard_map/fold_kernel/pallas_call | solution.py:427
  31.6 8.7 %collective-permute-done.3.got.got_b = f32[264,256]{1,0:T(8,128)S(1)} collective-permute-done((f32[264,256]{1,0:T(8,128)S(1)}, f32[264,256]{1,0:T(8,128)S(1)}, u32[]{:S(2)}, u32[]{:S(2)}) %collective-permute-start.3) | collective-permute-done | bytes 270368 | tf_op jit(solution)/shard_map/ppermute | solution.py:470
  40.4 1.2 collective-permute-start.4
  42.8 3.9 %fold_kernel.6 = (f32[520,256]{1,0:T(8,128)S(1)}, f32[264,256]{1,0:T(8,128)S(1)}) custom-call(s32[2]{0:T(128)S(1)} %pad_add_fusion.1.flags, s32[3]{0:T(128)S(1)} %pad_add_fusion.6.bits, f32[520,256]{1,0:T(8,128)S(1)} %get-tuple-element.37.state, f32[264,256]{1,0:T(8,128)S(1)} %collective-permute-done.3.got.got_b, ...), custom_call_target="tpu_custom_call", output_to_operand_aliasing={{0}: (2, {})} | custom-call | tf_op jit(solution)/shard_map/fold_kernel/pallas_call | solution.py:427
  47.0 6.4 %two_sides_kernel.2.sides = f32[2,520,256]{2,1,0:T(8,128)S(1)} custom-call(s32[2]{0:T(128)S(1)} %pad_add_fusion.1.flags, s32[3]{0:T(128)S(1)} %pad_add_fusion.6.bits, f32[2,520,256]{2,1,0:T(8,128)S(1)} %get-tuple-element.45.sides, f32[264,256]{1,0:T(8,128)S(1)} %collective-permute-done.1.got.got_a, ...), custom_call_target="tpu_custom_call", output_to_operand_aliasing={{}: (2, {})} | custom-call | tf_op jit(solution)/shard_map/two_sides_kernel/pallas_call | solution.py:427
  53.4 1.3 collective-permute-done.5.got.got_a
  57.0 3.9 %fold_kernel.7 = (f32[520,256]{1,0:T(8,128)S(1)}, f32[264,256]{1,0:T(8,128)S(1)}) custom-call(s32[2]{0:T(128)S(1)} %pad_add_fusion.1.flags, s32[3]{0:T(128)S(1)} %pad_add_fusion.5.bits, f32[520,256]{1,0:T(8,128)S(1)} %get-tuple-element.42.state, f32[264,256]{1,0:T(8,128)S(1)} %collective-permute-done.5.got.got_a, ...), custom_call_target="tpu_custom_call", output_to_operand_aliasing={{0}: (2, {})} | custom-call | tf_op jit(solution)/shard_map/fold_kernel/pallas_call | solution.py:427
  61.1 9.2 %collective-permute-done.7.got.got_b = f32[264,256]{1,0:T(8,128)S(1)} collective-permute-done((f32[264,256]{1,0:T(8,128)S(1)}, f32[264,256]{1,0:T(8,128)S(1)}, u32[]{:S(2)}, u32[]{:S(2)}) %collective-permute-start.7) | collective-permute-done | bytes 270368 | tf_op jit(solution)/shard_map/ppermute | solution.py:470
  70.2 1.2 collective-permute-start.8
  72.6 4.1 %fold_kernel.8 = (f32[520,256]{1,0:T(8,128)S(1)}, f32[264,256]{1,0:T(8,128)S(1)}) custom-call(s32[2]{0:T(128)S(1)} %pad_add_fusion.1.flags, s32[3]{0:T(128)S(1)} %pad_add_fusion.4.bits, f32[520,256]{1,0:T(8,128)S(1)} %get-tuple-element.47.state, f32[264,256]{1,0:T(8,128)S(1)} %collective-permute-done.7.got.got_b, ...), custom_call_target="tpu_custom_call", output_to_operand_aliasing={{0}: (2, {})} | custom-call | tf_op jit(solution)/shard_map/fold_kernel/pallas_call | solution.py:427
  76.9 7.3 %two_sides_kernel.3.sides = f32[2,520,256]{2,1,0:T(8,128)S(1)} custom-call(s32[2]{0:T(128)S(1)} %pad_add_fusion.1.flags, s32[3]{0:T(128)S(1)} %pad_add_fusion.4.bits, f32[2,520,256]{2,1,0:T(8,128)S(1)} %two_sides_kernel.2.sides, f32[264,256]{1,0:T(8,128)S(1)} %collective-permute-done.5.got.got_a, ...), custom_call_target="tpu_custom_call", output_to_operand_aliasing={{}: (2, {})} | custom-call | tf_op jit(solution)/shard_map/two_sides_kernel/pallas_call | solution.py:427
  86.9 4.4 %fold_kernel.9 = (f32[520,256]{1,0:T(8,128)S(1)}, f32[264,256]{1,0:T(8,128)S(1)}) custom-call(s32[2]{0:T(128)S(1)} %pad_add_fusion.1.flags, s32[3]{0:T(128)S(1)} %pad_add_fusion.3.bits, f32[520,256]{1,0:T(8,128)S(1)} %get-tuple-element.52.state, f32[264,256]{1,0:T(8,128)S(1)} %collective-permute-done.9.got, ...), custom_call_target="tpu_custom_call", output_to_operand_aliasing={{0}: (2, {})} | custom-call | tf_op jit(solution)/shard_map/fold_kernel/pallas_call | solution.py:427
  91.3 1.2 collective-permute-start.11
  92.6 4.4 %side_kernel.1.sides = f32[2,520,256]{2,1,0:T(8,128)S(1)} custom-call(s32[2]{0:T(128)S(1)} %pad_add_fusion.1.flags, s32[3]{0:T(128)S(1)} %pad_add_fusion.3.bits, f32[2,520,256]{2,1,0:T(8,128)S(1)} %two_sides_kernel.3.sides, f32[264,256]{1,0:T(8,128)S(1)} %collective-permute-done.9.got, ...), custom_call_target="tpu_custom_call", output_to_operand_aliasing={{}: (2, {})} | custom-call | tf_op jit(solution)/shard_map/side_kernel/pallas_call | solution.py:427
  96.9 9.0 %collective-permute-done.11.got = f32[264,256]{1,0:T(8,128)S(1)} collective-permute-done((f32[264,256]{1,0:T(8,128)S(1)}, f32[264,256]{1,0:T(8,128)S(1)}, u32[]{:S(2)}, u32[]{:S(2)}) %collective-permute-start.11) | collective-permute-done | bytes 270368 | tf_op jit(solution)/shard_map/ppermute | solution.py:470
  108.2 4.1 %edge_kernel.1 = f32[136,256]{1,0:T(8,128)S(1)} custom-call(s32[2]{0:T(128)S(1)} %pad_add_fusion.1.flags, s32[3]{0:T(128)S(1)} %pad_add_fusion.2.bits, f32[520,256]{1,0:T(8,128)S(1)} %get-tuple-element.57.state, f32[264,256]{1,0:T(8,128)S(1)} %collective-permute-done.11.got, f32[264,256]{1,0:T(8,128)S(1)} %collective-permute-done.12.far), custom_call_target="tpu_custom_call" | custom-call | tf_op jit(solution)/shard_map/edge_kernel/pallas_call | solution.py:427
  112.3 5.0 %collective-permute-start.13 = (f32[136,256]{1,0:T(8,128)S(1)}, f32[136,256]{1,0:T(8,128)S(1)}, u32[]{:S(2)}, u32[]{:S(2)}) collective-permute-start(f32[136,256]{1,0:T(8,128)S(1)} %edge_kernel.1), channel_id=1, source_target_pairs={{0,128},{1,129},{2,130},{3,131},{4,132},{5,133},{6,134},{7,135},{8... | collective-permute-start | bytes 417800 | tf_op jit(solution)/shard_map/ppermute | solution.py:470
  117.3 8.8 %close_kernel.1.closed = f32[520,256]{1,0:T(8,128)S(1)} custom-call(s32[2]{0:T(128)S(1)} %pad_add_fusion.1.flags, s32[3]{0:T(128)S(1)} %pad_add_fusion.2.bits, f32[2,520,256]{2,1,0:T(8,128)S(1)} %side_kernel.1.sides, f32[264,256]{1,0:T(8,128)S(1)} %collective-permute-done.11.got, f32[264,256]{1,0:T(8,128)S(1)} %collective-permute-done.12.far), custom_call_target="tpu_custom_call" | custom-call | tf_op jit(solution)/shard_map/close_kernel/pallas_call | solution.py:427
  126.1 4.4 %last_kernel.1 = (f32[1,256]{1,0:T(1,128)}, f32[1,256]{1,0:T(1,128)}) custom-call(s32[2]{0:T(128)S(1)} %pad_add_fusion.1.flags, s32[3]{0:T(128)S(1)} %pad_add_fusion.2.bits, f32[520,256]{1,0:T(8,128)S(1)} %close_kernel.1.closed, f32[136,256]{1,0:T(8,128)S(1)} %collective-permute-done.13.received), custom_call_target="tpu_custom_call" | custom-call | tf_op jit(solution)/shard_map/last_kernel/pallas_call | solution.py:427
  (30 shorter events, 16.5 us)
Async XLA Ops:
  2.8 1.0 copy-start
  3.7 0.9 copy-start.1
  8.3 5.1 %collective-permute-start = (f32[520,256]{1,0:T(8,128)S(1)}, f32[520,256]{1,0:T(8,128)S(1)}, u32[]{:S(2)}, u32[]{:S(2)}) collective-permute-start(f32[520,256]{1,0:T(8,128)S(1)} %build_kernel.1.mine), channel_id=1, source_target_pairs={{0,1},{1,0},{2,3},{3,2},{4,5},{5,4},{6,7},{7,6},{8,9},{9,8},{10,11... | collective-permute-start | bytes 1597448 | tf_op jit(solution)/shard_map/ppermute | solution.py:470
  17.3 7.8 %collective-permute-start.1 = (f32[264,256]{1,0:T(8,128)S(1)}, f32[264,256]{1,0:T(8,128)S(1)}, u32[]{:S(2)}, u32[]{:S(2)}) collective-permute-start(f32[264,256]{1,0:T(8,128)S(1)} %get-tuple-element.34), channel_id=1, source_target_pairs={{0,2},{1,3},{2,0},{3,1},{4,6},{5,7},{6,4},{7,5},{8,10},{9,11},{10,... | collective-permute-start | bytes 811016 | tf_op jit(solution)/shard_map/ppermute | solution.py:470
  25.1 2.4 %collective-permute-start.2 = (f32[264,256]{1,0:T(8,128)S(1)}, f32[264,256]{1,0:T(8,128)S(1)}, u32[]{:S(2)}, u32[]{:S(2)}) collective-permute-start(f32[264,256]{1,0:T(8,128)S(1)} %collective-permute-done.1.got.got_a), channel_id=1, source_target_pairs={{0,1},{1,0},{2,3},{3,2},{4,5},{5,4},{6,7},{7,6},{8,9},{9,8},{10,11... | collective-permute-start | bytes 811016 | tf_op jit(solution)/shard_map/ppermute | solution.py:470
  31.1 9.2 %collective-permute-start.3 = (f32[264,256]{1,0:T(8,128)S(1)}, f32[264,256]{1,0:T(8,128)S(1)}, u32[]{:S(2)}, u32[]{:S(2)}) collective-permute-start(f32[264,256]{1,0:T(8,128)S(1)} %get-tuple-element.38), channel_id=1, source_target_pairs={{0,4},{1,5},{2,6},{3,7},{4,0},{5,1},{6,2},{7,3},{8,12},{9,13},{10,... | collective-permute-start | bytes 811016 | tf_op jit(solution)/shard_map/ppermute | solution.py:470
  40.4 2.4 %collective-permute-start.4 = (f32[264,256]{1,0:T(8,128)S(1)}, f32[264,256]{1,0:T(8,128)S(1)}, u32[]{:S(2)}, u32[]{:S(2)}) collective-permute-start(f32[264,256]{1,0:T(8,128)S(1)} %collective-permute-done.3.got.got_b), channel_id=1, source_target_pairs={{0,1},{1,0},{2,3},{3,2},{4,5},{5,4},{6,7},{7,6},{8,9},{9,8},{10,11... | collective-permute-start | bytes 811016 | tf_op jit(solution)/shard_map/ppermute | solution.py:470
  46.7 8.0 %collective-permute-start.5 = (f32[264,256]{1,0:T(8,128)S(1)}, f32[264,256]{1,0:T(8,128)S(1)}, u32[]{:S(2)}, u32[]{:S(2)}) collective-permute-start(f32[264,256]{1,0:T(8,128)S(1)} %get-tuple-element.43), channel_id=1, source_target_pairs={{0,8},{1,9},{2,10},{3,11},{4,12},{5,13},{6,14},{7,15},{8,0},{9,1},... | collective-permute-start | bytes 811016 | tf_op jit(solution)/shard_map/ppermute | solution.py:470
  54.7 2.4 %collective-permute-start.6 = (f32[264,256]{1,0:T(8,128)S(1)}, f32[264,256]{1,0:T(8,128)S(1)}, u32[]{:S(2)}, u32[]{:S(2)}) collective-permute-start(f32[264,256]{1,0:T(8,128)S(1)} %collective-permute-done.5.got.got_a), channel_id=1, source_target_pairs={{0,1},{1,0},{2,3},{3,2},{4,5},{5,4},{6,7},{7,6},{8,9},{9,8},{10,11... | collective-permute-start | bytes 811016 | tf_op jit(solution)/shard_map/ppermute | solution.py:470
  61.0 9.3 %collective-permute-start.7 = (f32[264,256]{1,0:T(8,128)S(1)}, f32[264,256]{1,0:T(8,128)S(1)}, u32[]{:S(2)}, u32[]{:S(2)}) collective-permute-start(f32[264,256]{1,0:T(8,128)S(1)} %get-tuple-element.48), channel_id=1, source_target_pairs={{0,16},{1,17},{2,18},{3,19},{4,20},{5,21},{6,22},{7,23},{8,24},{9,... | collective-permute-start | bytes 811016 | tf_op jit(solution)/shard_map/ppermute | solution.py:470
  70.2 2.4 %collective-permute-start.8 = (f32[264,256]{1,0:T(8,128)S(1)}, f32[264,256]{1,0:T(8,128)S(1)}, u32[]{:S(2)}, u32[]{:S(2)}) collective-permute-start(f32[264,256]{1,0:T(8,128)S(1)} %collective-permute-done.7.got.got_b), channel_id=1, source_target_pairs={{0,1},{1,0},{2,3},{3,2},{4,5},{5,4},{6,7},{7,6},{8,9},{9,8},{10,11... | collective-permute-start | bytes 811016 | tf_op jit(solution)/shard_map/ppermute | solution.py:470
  76.8 7.8 %collective-permute-start.9 = (f32[264,256]{1,0:T(8,128)S(1)}, f32[264,256]{1,0:T(8,128)S(1)}, u32[]{:S(2)}, u32[]{:S(2)}) collective-permute-start(f32[264,256]{1,0:T(8,128)S(1)} %get-tuple-element.53), channel_id=1, source_target_pairs={{0,32},{1,33},{2,34},{3,35},{4,36},{5,37},{6,38},{7,39},{8,40},{9,... | collective-permute-start | bytes 811016 | tf_op jit(solution)/shard_map/ppermute | solution.py:470
  84.5 2.4 %collective-permute-start.10 = (f32[264,256]{1,0:T(8,128)S(1)}, f32[264,256]{1,0:T(8,128)S(1)}, u32[]{:S(2)}, u32[]{:S(2)}) collective-permute-start(f32[264,256]{1,0:T(8,128)S(1)} %collective-permute-done.9.got), channel_id=1, source_target_pairs={{0,1},{1,0},{2,3},{3,2},{4,5},{5,4},{6,7},{7,6},{8,9},{9,8},{10,11... | collective-permute-start | bytes 811016 | tf_op jit(solution)/shard_map/ppermute | solution.py:470
  91.3 14.6 %collective-permute-start.11 = (f32[264,256]{1,0:T(8,128)S(1)}, f32[264,256]{1,0:T(8,128)S(1)}, u32[]{:S(2)}, u32[]{:S(2)}) collective-permute-start(f32[264,256]{1,0:T(8,128)S(1)} %get-tuple-element.58), channel_id=1, source_target_pairs={{0,64},{1,65},{2,66},{3,67},{4,68},{5,69},{6,70},{7,71},{8,72},{9,... | collective-permute-start | bytes 811016 | tf_op jit(solution)/shard_map/ppermute | solution.py:470
  105.9 2.3 %collective-permute-start.12 = (f32[264,256]{1,0:T(8,128)S(1)}, f32[264,256]{1,0:T(8,128)S(1)}, u32[]{:S(2)}, u32[]{:S(2)}) collective-permute-start(f32[264,256]{1,0:T(8,128)S(1)} %collective-permute-done.11.got), channel_id=1, source_target_pairs={{0,1},{1,0},{2,3},{3,2},{4,5},{5,4},{6,7},{7,6},{8,9},{9,8},{10,11... | collective-permute-start | bytes 811016 | tf_op jit(solution)/shard_map/ppermute | solution.py:470
  112.3 13.8 %collective-permute-start.13 = (f32[136,256]{1,0:T(8,128)S(1)}, f32[136,256]{1,0:T(8,128)S(1)}, u32[]{:S(2)}, u32[]{:S(2)}) collective-permute-start(f32[136,256]{1,0:T(8,128)S(1)} %edge_kernel.1), channel_id=1, source_target_pairs={{0,128},{1,129},{2,130},{3,131},{4,132},{5,133},{6,134},{7,135},{8... | collective-permute-start | bytes 417800 | tf_op jit(solution)/shard_map/ppermute | solution.py:470
